TPU v7x, 32 devices: a whole 2x2x4 slice. The times are simulated.
32 devices in a mesh: gx: 8 (over z, x), af: 4 (over y, core).
Axes of the slice: x: 2, y: 2, z: 4, core: 2. Of those that a mesh axis runs over, the one named last changes fastest.
Arguments:
- forcing: float32 [16, 2, 32, 5, 4, 256], P('af', None, 'gx'), may hold values from -6 to 6
- flow: float32 [32, 4, 256], P('gx'), may hold values from 0.2 to 1
- sponge: float32 [32, 4, 256], P('gx'), may hold values from 0.05 to 0.5
- coupling: float32 [5, 5], replicated, may hold values from -1.5 to 1.5
- omega: float32 [2], replicated, may hold values from 1 to 1.6
Outputs:
- basis: float32 [16, 2, 32, 5, 4, 256], P('af', None, 'gx')
- coeff: float32 [16, 16], replicated
All inputs are finite; a program needn't handle non-finite values.
Results may differ from a plain program's by a relative error of at most 0.0001.
Values sent between devices are 32-bit elements; how exact they have to be, the bound alone decides.
No kernel may reach another device: no remote copies, remote signals or barrier semaphores. Data moves between devices by JAX's collectives and lax.ppermute only.
A program may use at most 64 MiB of HBM per device.

v0:
```python
import jax
import jax.numpy as jnp
from jax import lax
from jax.sharding import PartitionSpec as P

FORCINGS = 8
SWEEPS = 8
viscosity = 0.25


def padded_2(array, sides, width):
    for axis, dim in sides:
        size, length = (lax.axis_size(axis), array.shape[dim])
        up = [(i, (i + 1) % size) for i in range(size - 1)]
        down = [(j, i) for i, j in up]
        last = lax.slice_in_dim(array, length - width, length, axis=dim)
        leading = lax.slice_in_dim(array, 0, width, axis=dim)
        before = lax.ppermute(last, axis, up)
        after = lax.ppermute(leading, axis, down)
        array = jnp.concatenate([before, array, after], axis=dim)
    return array


def apply_adjoint(padded, freq, flow, sponge, coupling):
    field = padded[:, :, 1:-1]
    upper = padded[:, :, 2:]
    lower = padded[:, :, :-2]
    radial = jnp.pad(field, ((0, 0), (0, 0), (0, 0), (0, 0), (1, 1), (0, 0)))
    lap = upper + lower + radial[:, :, :, :, 2:, :] + radial[:, :, :, :, :-2, :]
    lap = lap + jnp.roll(field, 1, -1) + jnp.roll(field, -1, -1) - 6.0 * field
    advect = 0.5 * flow[None, None, :, None] * (lower - upper)
    mixed = jnp.einsum("wv,kpxwrt->kpxvrt", coupling, field, precision=lax.Precision.HIGHEST)
    rotate = jnp.stack([freq * field[:, 1], -freq * field[:, 0]], axis=1)
    return sponge[None, None, :, None] * field + rotate - mixed + advect - viscosity * lap


def precondition(resid, freq, sponge, coupling):
    diag_re = sponge[:, None] + 6.0 * viscosity - jnp.diagonal(coupling)[None, :, None, None]
    diag_re = diag_re[None]
    denom = diag_re * diag_re + freq * freq
    p_re = diag_re / denom
    p_im = freq / denom
    part_re = p_re * resid[:, 0] - p_im * resid[:, 1]
    part_im = p_re * resid[:, 1] + p_im * resid[:, 0]
    return jnp.stack([part_re, part_im], axis=1)


def with_faces(field):
    return padded_2(field, (("gx", 2),), 1)


def on_device(forcing, flow, sponge, coupling, omega):
    local_cols = forcing.shape[0]
    column_ids = lax.axis_index("af") * local_cols + jnp.arange(local_cols)
    freq_vec = jnp.where(column_ids < FORCINGS, omega[0], omega[1])
    freq_b = freq_vec[:, None, None, None, None]
    field = precondition(forcing, freq_b, sponge, coupling)
    for sweep in range(SWEEPS):
        padded = with_faces(field)
        image = apply_adjoint(padded, freq_b, flow, sponge, coupling)
        field = field + precondition(forcing - image, freq_b, sponge, coupling)
    all_cols = local_cols * lax.axis_size("af")
    eye_matrix = jnp.eye(all_cols, dtype=jnp.float32)
    regrouped = lax.all_to_all(field, "af", split_axis=4, concat_axis=0, tiled=True)
    flat = regrouped.reshape(all_cols, -1)
    total = flat.shape[1] * lax.axis_size("gx") * lax.axis_size("af")
    local_gram = jnp.dot(flat, flat.T, precision=lax.Precision.HIGHEST)
    partial_gram = lax.psum(local_gram, "af")
    gram = lax.psum(partial_gram, "gx")
    lower_factor = jnp.linalg.cholesky(gram)
    inverse = jax.scipy.linalg.solve_triangular(lower_factor, eye_matrix, lower=True)
    scaled = jnp.dot(inverse, flat, precision=lax.Precision.HIGHEST) * jnp.sqrt(jnp.float32(total))
    basis = lax.all_to_all(
        scaled.reshape(regrouped.shape), "af", split_axis=0, concat_axis=4, tiled=True
    )
    coeff = lower_factor.T / jnp.sqrt(jnp.float32(total))
    return (basis, coeff)


def solution(mesh):
    placed = (
        P("af", None, "gx", None, None, None),
        P("gx", None, None),
        P("gx", None, None),
        P(),
        P(),
    )
    return jax.shard_map(
        on_device,
        mesh=mesh,
        in_specs=placed,
        out_specs=(P("af", None, "gx", None, None, None), P()),
        check_vma=False,
    )
```

profile of v0, /device:TPU:0, one launch (start us, length us, event | category | flops | bytes accessed | tf_op | source)
XLA Modules:
  0.0 230.4 jit_solution(16400706654534699275)
XLA Ops:
  7.8 5.5 %collective-permute-start = (f32[4,2,1,5,4,256]{5,3,4,2,1,0:T(8,128)S(1)}, f32[4,2,1,5,4,256]{5,3,4,2,1,0:T(8,128)S(1)}, u32[]{:S(2)}, u32[]{:S(2)}) collective-permute-start(f32[4,2,1,5,4,256]{5,3,4,2,1,0:T(8,128)S(1)} %get-tuple-element.89), channel_id=1, source_target_pairs={{0,4},{4,8},{8,12},{12,16},{16,20},{20,24},{24,28},{1,5},{5,9},{9,... | collective-permute-start | bytes 491528 | tf_op jit(solution)/shard_map/ppermute | solution.py:18
  17.6 5.8 %collective-permute-done = f32[4,2,1,5,4,256]{5,3,4,2,1,0:T(8,128)S(1)} collective-permute-done((f32[4,2,1,5,4,256]{5,3,4,2,1,0:T(8,128)S(1)}, f32[4,2,1,5,4,256]{5,3,4,2,1,0:T(8,128)S(1)}, u32[]{:S(2)}, u32[]{:S(2)}) %collective-permute-start) | collective-permute-done | bytes 163872 | tf_op jit(solution)/shard_map/ppermute | solution.py:18
  27.9 5.0 %collective-permute-start.2 = (f32[4,2,1,5,4,256]{5,3,4,2,1,0:T(8,128)S(1)}, f32[4,2,1,5,4,256]{5,3,4,2,1,0:T(8,128)S(1)}, u32[]{:S(2)}, u32[]{:S(2)}) collective-permute-start(f32[4,2,1,5,4,256]{5,3,4,2,1,0:T(8,128)S(1)} %get-tuple-element.83), channel_id=1, source_target_pairs={{0,4},{4,8},{8,12},{12,16},{16,20},{20,24},{24,28},{1,5},{5,9},{9,... | collective-permute-start | bytes 491528 | tf_op jit(solution)/shard_map/ppermute | solution.py:18
  37.5 5.8 %collective-permute-done.2 = f32[4,2,1,5,4,256]{5,3,4,2,1,0:T(8,128)S(1)} collective-permute-done((f32[4,2,1,5,4,256]{5,3,4,2,1,0:T(8,128)S(1)}, f32[4,2,1,5,4,256]{5,3,4,2,1,0:T(8,128)S(1)}, u32[]{:S(2)}, u32[]{:S(2)}) %collective-permute-start.2) | collective-permute-done | bytes 163872 | tf_op jit(solution)/shard_map/ppermute | solution.py:18
  47.9 5.0 %collective-permute-start.4 = (f32[4,2,1,5,4,256]{5,3,4,2,1,0:T(8,128)S(1)}, f32[4,2,1,5,4,256]{5,3,4,2,1,0:T(8,128)S(1)}, u32[]{:S(2)}, u32[]{:S(2)}) collective-permute-start(f32[4,2,1,5,4,256]{5,3,4,2,1,0:T(8,128)S(1)} %get-tuple-element.75), channel_id=1, source_target_pairs={{0,4},{4,8},{8,12},{12,16},{16,20},{20,24},{24,28},{1,5},{5,9},{9,... | collective-permute-start | bytes 491528 | tf_op jit(solution)/shard_map/ppermute | solution.py:18
  53.1 4.3 %collective-permute-done.5 = f32[4,2,1,5,4,256]{5,3,4,2,1,0:T(8,128)S(1)} collective-permute-done((f32[4,2,1,5,4,256]{5,3,4,2,1,0:T(8,128)S(1)}, f32[4,2,1,5,4,256]{5,3,4,2,1,0:T(8,128)S(1)}, u32[]{:S(2)}, u32[]{:S(2)}) %collective-permute-start.5) | collective-permute-done | bytes 163872 | tf_op jit(solution)/shard_map/ppermute | solution.py:19
  57.5 5.8 %collective-permute-done.4 = f32[4,2,1,5,4,256]{5,3,4,2,1,0:T(8,128)S(1)} collective-permute-done((f32[4,2,1,5,4,256]{5,3,4,2,1,0:T(8,128)S(1)}, f32[4,2,1,5,4,256]{5,3,4,2,1,0:T(8,128)S(1)}, u32[]{:S(2)}, u32[]{:S(2)}) %collective-permute-start.4) | collective-permute-done | bytes 163872 | tf_op jit(solution)/shard_map/ppermute | solution.py:18
  68.0 5.2 %collective-permute-start.6 = (f32[4,2,1,5,4,256]{5,3,4,2,1,0:T(8,128)S(1)}, f32[4,2,1,5,4,256]{5,3,4,2,1,0:T(8,128)S(1)}, u32[]{:S(2)}, u32[]{:S(2)}) collective-permute-start(f32[4,2,1,5,4,256]{5,3,4,2,1,0:T(8,128)S(1)} %get-tuple-element.67), channel_id=1, source_target_pairs={{0,4},{4,8},{8,12},{12,16},{16,20},{20,24},{24,28},{1,5},{5,9},{9,... | collective-permute-start | bytes 491528 | tf_op jit(solution)/shard_map/ppermute | solution.py:18
  77.6 5.8 %collective-permute-done.6 = f32[4,2,1,5,4,256]{5,3,4,2,1,0:T(8,128)S(1)} collective-permute-done((f32[4,2,1,5,4,256]{5,3,4,2,1,0:T(8,128)S(1)}, f32[4,2,1,5,4,256]{5,3,4,2,1,0:T(8,128)S(1)}, u32[]{:S(2)}, u32[]{:S(2)}) %collective-permute-start.6) | collective-permute-done | bytes 163872 | tf_op jit(solution)/shard_map/ppermute | solution.py:18
  88.2 5.0 %collective-permute-start.8 = (f32[4,2,1,5,4,256]{5,3,4,2,1,0:T(8,128)S(1)}, f32[4,2,1,5,4,256]{5,3,4,2,1,0:T(8,128)S(1)}, u32[]{:S(2)}, u32[]{:S(2)}) collective-permute-start(f32[4,2,1,5,4,256]{5,3,4,2,1,0:T(8,128)S(1)} %get-tuple-element.59), channel_id=1, source_target_pairs={{0,4},{4,8},{8,12},{12,16},{16,20},{20,24},{24,28},{1,5},{5,9},{9,... | collective-permute-start | bytes 491528 | tf_op jit(solution)/shard_map/ppermute | solution.py:18
  93.5 4.3 %collective-permute-done.9 = f32[4,2,1,5,4,256]{5,3,4,2,1,0:T(8,128)S(1)} collective-permute-done((f32[4,2,1,5,4,256]{5,3,4,2,1,0:T(8,128)S(1)}, f32[4,2,1,5,4,256]{5,3,4,2,1,0:T(8,128)S(1)}, u32[]{:S(2)}, u32[]{:S(2)}) %collective-permute-start.9) | collective-permute-done | bytes 163872 | tf_op jit(solution)/shard_map/ppermute | solution.py:19
  97.8 5.8 %collective-permute-done.8 = f32[4,2,1,5,4,256]{5,3,4,2,1,0:T(8,128)S(1)} collective-permute-done((f32[4,2,1,5,4,256]{5,3,4,2,1,0:T(8,128)S(1)}, f32[4,2,1,5,4,256]{5,3,4,2,1,0:T(8,128)S(1)}, u32[]{:S(2)}, u32[]{:S(2)}) %collective-permute-start.8) | collective-permute-done | bytes 163872 | tf_op jit(solution)/shard_map/ppermute | solution.py:18
  108.6 5.0 %collective-permute-start.10 = (f32[4,2,1,5,4,256]{5,3,4,2,1,0:T(8,128)S(1)}, f32[4,2,1,5,4,256]{5,3,4,2,1,0:T(8,128)S(1)}, u32[]{:S(2)}, u32[]{:S(2)}) collective-permute-start(f32[4,2,1,5,4,256]{5,3,4,2,1,0:T(8,128)S(1)} %get-tuple-element.51), channel_id=1, source_target_pairs={{0,4},{4,8},{8,12},{12,16},{16,20},{20,24},{24,28},{1,5},{5,9},{9,... | collective-permute-start | bytes 491528 | tf_op jit(solution)/shard_map/ppermute | solution.py:18
  113.8 4.3 %collective-permute-done.11 = f32[4,2,1,5,4,256]{5,3,4,2,1,0:T(8,128)S(1)} collective-permute-done((f32[4,2,1,5,4,256]{5,3,4,2,1,0:T(8,128)S(1)}, f32[4,2,1,5,4,256]{5,3,4,2,1,0:T(8,128)S(1)}, u32[]{:S(2)}, u32[]{:S(2)}) %collective-permute-start.11) | collective-permute-done | bytes 163872 | tf_op jit(solution)/shard_map/ppermute | solution.py:19
  118.1 5.8 %collective-permute-done.10 = f32[4,2,1,5,4,256]{5,3,4,2,1,0:T(8,128)S(1)} collective-permute-done((f32[4,2,1,5,4,256]{5,3,4,2,1,0:T(8,128)S(1)}, f32[4,2,1,5,4,256]{5,3,4,2,1,0:T(8,128)S(1)}, u32[]{:S(2)}, u32[]{:S(2)}) %collective-permute-start.10) | collective-permute-done | bytes 163872 | tf_op jit(solution)/shard_map/ppermute | solution.py:18
  129.0 5.2 %collective-permute-start.12 = (f32[4,2,1,5,4,256]{5,3,4,2,1,0:T(8,128)S(1)}, f32[4,2,1,5,4,256]{5,3,4,2,1,0:T(8,128)S(1)}, u32[]{:S(2)}, u32[]{:S(2)}) collective-permute-start(f32[4,2,1,5,4,256]{5,3,4,2,1,0:T(8,128)S(1)} %get-tuple-element.43), channel_id=1, source_target_pairs={{0,4},{4,8},{8,12},{12,16},{16,20},{20,24},{24,28},{1,5},{5,9},{9,... | collective-permute-start | bytes 491528 | tf_op jit(solution)/shard_map/ppermute | solution.py:18
  138.6 5.8 %collective-permute-done.12 = f32[4,2,1,5,4,256]{5,3,4,2,1,0:T(8,128)S(1)} collective-permute-done((f32[4,2,1,5,4,256]{5,3,4,2,1,0:T(8,128)S(1)}, f32[4,2,1,5,4,256]{5,3,4,2,1,0:T(8,128)S(1)}, u32[]{:S(2)}, u32[]{:S(2)}) %collective-permute-start.12) | collective-permute-done | bytes 163872 | tf_op jit(solution)/shard_map/ppermute | solution.py:18
  149.5 5.0 %collective-permute-start.14 = (f32[4,2,1,5,4,256]{5,3,4,2,1,0:T(8,128)S(1)}, f32[4,2,1,5,4,256]{5,3,4,2,1,0:T(8,128)S(1)}, u32[]{:S(2)}, u32[]{:S(2)}) collective-permute-start(f32[4,2,1,5,4,256]{5,3,4,2,1,0:T(8,128)S(1)} %get-tuple-element.35), channel_id=1, source_target_pairs={{0,4},{4,8},{8,12},{12,16},{16,20},{20,24},{24,28},{1,5},{5,9},{9,... | collective-permute-start | bytes 491528 | tf_op jit(solution)/shard_map/ppermute | solution.py:18
  154.8 4.3 %collective-permute-done.15 = f32[4,2,1,5,4,256]{5,3,4,2,1,0:T(8,128)S(1)} collective-permute-done((f32[4,2,1,5,4,256]{5,3,4,2,1,0:T(8,128)S(1)}, f32[4,2,1,5,4,256]{5,3,4,2,1,0:T(8,128)S(1)}, u32[]{:S(2)}, u32[]{:S(2)}) %collective-permute-start.15) | collective-permute-done | bytes 163872 | tf_op jit(solution)/shard_map/ppermute | solution.py:19
  159.1 5.8 %collective-permute-done.14 = f32[4,2,1,5,4,256]{5,3,4,2,1,0:T(8,128)S(1)} collective-permute-done((f32[4,2,1,5,4,256]{5,3,4,2,1,0:T(8,128)S(1)}, f32[4,2,1,5,4,256]{5,3,4,2,1,0:T(8,128)S(1)}, u32[]{:S(2)}, u32[]{:S(2)}) %collective-permute-start.14) | collective-permute-done | bytes 163872 | tf_op jit(solution)/shard_map/ppermute | solution.py:18
  168.9 12.8 %all_to_all.33 = f32[4,2,4,5,4,256]{5,2,3,1,0,4:T(4,128)S(1)} all-to-all(f32[4,2,4,5,4,256]{5,2,3,1,0,4:T(4,128)S(1)} %copy.46), channel_id=1, replica_groups=mesh['gx'=8,'af'=4] {'af'}, dimensions={4} | all-to-all | bytes 1310720 | tf_op jit(solution)/shard_map/all_to_all | solution.py:64
  183.1 5.9 %psum.14 = f32[16,16]{0,1:T(8,128)S(1)} all-reduce(f32[16,16]{0,1:T(8,128)S(1)} %fusion.105), channel_id=1, replica_groups=mesh['gx'=8,'af'=4] {'af'}, use_global_device_ids=true, to_apply=%region_0.1 | all-reduce | flops 256 | bytes 2048 | tf_op jit(solution)/shard_map/psum | solution.py:68
  189.0 20.1 %psum.15 = f32[16,16]{0,1:T(8,128)S(1)} all-reduce(f32[16,16]{0,1:T(8,128)S(1)} %psum.14), channel_id=1, replica_groups=mesh['gx'=8,'af'=4] {'gx'}, use_global_device_ids=true, to_apply=%region_1.2 | all-reduce | flops 256 | bytes 2048 | tf_op jit(solution)/shard_map/psum | solution.py:69
  219.7 9.5 %all-to-all-done.1 = f32[16,2,4,5,1,256]{5,2,4,3,1,0:T(4,128)S(1)} async-done(((f32[16,2,4,5,1,256]{5,2,4,3,1,0:T(4,128)}), f32[16,2,4,5,1,256]{5,2,4,3,1,0:T(4,128)S(1)}, u32[]{:S(2)}, u32[]{:S(2)}) %all-to-all-start.1) | async-done | bytes 655392 | tf_op jit(solution)/shard_map/all_to_all | solution.py:73
  (104 shorter events, 76.3 us)
Async XLA Ops:
  0.6 4.7 %copy-start = (f32[5,5]{1,0:T(8,128)S(1)}, f32[5,5]{1,0:T(8,128)}, u32[]{:S(2)}) copy-start(f32[5,5]{1,0:T(8,128)} %param.8) | copy-start | bytes 304
  6.5 11.2 %collective-permute-start.1 = (f32[4,2,1,5,4,256]{5,3,4,2,1,0:T(8,128)S(1)}, f32[4,2,1,5,4,256]{5,3,4,2,1,0:T(8,128)S(1)}, u32[]{:S(2)}, u32[]{:S(2)}) collective-permute-start(f32[4,2,1,5,4,256]{5,3,4,2,1,0:T(8,128)S(1)} %get-tuple-element.88), channel_id=1, source_target_pairs={{4,0},{8,4},{12,8},{16,12},{20,16},{24,20},{28,24},{5,1},{9,5},{13... | collective-permute-start | bytes 491528 | tf_op jit(solution)/shard_map/ppermute | solution.py:19
  7.8 15.6 %collective-permute-start = (f32[4,2,1,5,4,256]{5,3,4,2,1,0:T(8,128)S(1)}, f32[4,2,1,5,4,256]{5,3,4,2,1,0:T(8,128)S(1)}, u32[]{:S(2)}, u32[]{:S(2)}) collective-permute-start(f32[4,2,1,5,4,256]{5,3,4,2,1,0:T(8,128)S(1)} %get-tuple-element.89), channel_id=1, source_target_pairs={{0,4},{4,8},{8,12},{12,16},{16,20},{20,24},{24,28},{1,5},{5,9},{9,... | collective-permute-start | bytes 491528 | tf_op jit(solution)/shard_map/ppermute | solution.py:18
  13.4 0.7 copy-start.2
  14.1 9.3 %copy-start.1 = (f32[4,2,4,5,4,256]{5,4,3,2,1,0:T(4,128)S(1)}, f32[4,2,4,5,4,256]{5,4,3,2,1,0:T(4,128)}, u32[]{:S(2)}) copy-start(f32[4,2,4,5,4,256]{5,4,3,2,1,0:T(4,128)} %param.5) | copy-start | bytes 1966084
  14.1 9.3 %copy-start.3 = (f32[4,4,256]{2,1,0:T(4,128)S(1)}, f32[4,4,256]{2,1,0:T(4,128)}, u32[]{:S(2)}) copy-start(f32[4,4,256]{2,1,0:T(4,128)} %param.7) | copy-start | bytes 49156
  26.6 10.9 %collective-permute-start.3 = (f32[4,2,1,5,4,256]{5,3,4,2,1,0:T(8,128)S(1)}, f32[4,2,1,5,4,256]{5,3,4,2,1,0:T(8,128)S(1)}, u32[]{:S(2)}, u32[]{:S(2)}) collective-permute-start(f32[4,2,1,5,4,256]{5,3,4,2,1,0:T(8,128)S(1)} %get-tuple-element.82), channel_id=1, source_target_pairs={{4,0},{8,4},{12,8},{16,12},{20,16},{24,20},{28,24},{5,1},{9,5},{13... | collective-permute-start | bytes 491528 | tf_op jit(solution)/shard_map/ppermute | solution.py:19
  27.9 15.3 %collective-permute-start.2 = (f32[4,2,1,5,4,256]{5,3,4,2,1,0:T(8,128)S(1)}, f32[4,2,1,5,4,256]{5,3,4,2,1,0:T(8,128)S(1)}, u32[]{:S(2)}, u32[]{:S(2)}) collective-permute-start(f32[4,2,1,5,4,256]{5,3,4,2,1,0:T(8,128)S(1)} %get-tuple-element.83), channel_id=1, source_target_pairs={{0,4},{4,8},{8,12},{12,16},{16,20},{20,24},{24,28},{1,5},{5,9},{9,... | collective-permute-start | bytes 491528 | tf_op jit(solution)/shard_map/ppermute | solution.py:18
  46.6 10.9 %collective-permute-start.5 = (f32[4,2,1,5,4,256]{5,3,4,2,1,0:T(8,128)S(1)}, f32[4,2,1,5,4,256]{5,3,4,2,1,0:T(8,128)S(1)}, u32[]{:S(2)}, u32[]{:S(2)}) collective-permute-start(f32[4,2,1,5,4,256]{5,3,4,2,1,0:T(8,128)S(1)} %get-tuple-element.74), channel_id=1, source_target_pairs={{4,0},{8,4},{12,8},{16,12},{20,16},{24,20},{28,24},{5,1},{9,5},{13... | collective-permute-start | bytes 491528 | tf_op jit(solution)/shard_map/ppermute | solution.py:19
  47.9 15.3 %collective-permute-start.4 = (f32[4,2,1,5,4,256]{5,3,4,2,1,0:T(8,128)S(1)}, f32[4,2,1,5,4,256]{5,3,4,2,1,0:T(8,128)S(1)}, u32[]{:S(2)}, u32[]{:S(2)}) collective-permute-start(f32[4,2,1,5,4,256]{5,3,4,2,1,0:T(8,128)S(1)} %get-tuple-element.75), channel_id=1, source_target_pairs={{0,4},{4,8},{8,12},{12,16},{16,20},{20,24},{24,28},{1,5},{5,9},{9,... | collective-permute-start | bytes 491528 | tf_op jit(solution)/shard_map/ppermute | solution.py:18
  66.7 10.9 %collective-permute-start.7 = (f32[4,2,1,5,4,256]{5,3,4,2,1,0:T(8,128)S(1)}, f32[4,2,1,5,4,256]{5,3,4,2,1,0:T(8,128)S(1)}, u32[]{:S(2)}, u32[]{:S(2)}) collective-permute-start(f32[4,2,1,5,4,256]{5,3,4,2,1,0:T(8,128)S(1)} %get-tuple-element.66), channel_id=1, source_target_pairs={{4,0},{8,4},{12,8},{16,12},{20,16},{24,20},{28,24},{5,1},{9,5},{13... | collective-permute-start | bytes 491528 | tf_op jit(solution)/shard_map/ppermute | solution.py:19
  68.0 15.3 %collective-permute-start.6 = (f32[4,2,1,5,4,256]{5,3,4,2,1,0:T(8,128)S(1)}, f32[4,2,1,5,4,256]{5,3,4,2,1,0:T(8,128)S(1)}, u32[]{:S(2)}, u32[]{:S(2)}) collective-permute-start(f32[4,2,1,5,4,256]{5,3,4,2,1,0:T(8,128)S(1)} %get-tuple-element.67), channel_id=1, source_target_pairs={{0,4},{4,8},{8,12},{12,16},{16,20},{20,24},{24,28},{1,5},{5,9},{9,... | collective-permute-start | bytes 491528 | tf_op jit(solution)/shard_map/ppermute | solution.py:18
  86.9 10.9 %collective-permute-start.9 = (f32[4,2,1,5,4,256]{5,3,4,2,1,0:T(8,128)S(1)}, f32[4,2,1,5,4,256]{5,3,4,2,1,0:T(8,128)S(1)}, u32[]{:S(2)}, u32[]{:S(2)}) collective-permute-start(f32[4,2,1,5,4,256]{5,3,4,2,1,0:T(8,128)S(1)} %get-tuple-element.58), channel_id=1, source_target_pairs={{4,0},{8,4},{12,8},{16,12},{20,16},{24,20},{28,24},{5,1},{9,5},{13... | collective-permute-start | bytes 491528 | tf_op jit(solution)/shard_map/ppermute | solution.py:19
  88.2 15.3 %collective-permute-start.8 = (f32[4,2,1,5,4,256]{5,3,4,2,1,0:T(8,128)S(1)}, f32[4,2,1,5,4,256]{5,3,4,2,1,0:T(8,128)S(1)}, u32[]{:S(2)}, u32[]{:S(2)}) collective-permute-start(f32[4,2,1,5,4,256]{5,3,4,2,1,0:T(8,128)S(1)} %get-tuple-element.59), channel_id=1, source_target_pairs={{0,4},{4,8},{8,12},{12,16},{16,20},{20,24},{24,28},{1,5},{5,9},{9,... | collective-permute-start | bytes 491528 | tf_op jit(solution)/shard_map/ppermute | solution.py:18
  107.3 10.9 %collective-permute-start.11 = (f32[4,2,1,5,4,256]{5,3,4,2,1,0:T(8,128)S(1)}, f32[4,2,1,5,4,256]{5,3,4,2,1,0:T(8,128)S(1)}, u32[]{:S(2)}, u32[]{:S(2)}) collective-permute-start(f32[4,2,1,5,4,256]{5,3,4,2,1,0:T(8,128)S(1)} %get-tuple-element.50), channel_id=1, source_target_pairs={{4,0},{8,4},{12,8},{16,12},{20,16},{24,20},{28,24},{5,1},{9,5},{13... | collective-permute-start | bytes 491528 | tf_op jit(solution)/shard_map/ppermute | solution.py:19
  108.6 15.3 %collective-permute-start.10 = (f32[4,2,1,5,4,256]{5,3,4,2,1,0:T(8,128)S(1)}, f32[4,2,1,5,4,256]{5,3,4,2,1,0:T(8,128)S(1)}, u32[]{:S(2)}, u32[]{:S(2)}) collective-permute-start(f32[4,2,1,5,4,256]{5,3,4,2,1,0:T(8,128)S(1)} %get-tuple-element.51), channel_id=1, source_target_pairs={{0,4},{4,8},{8,12},{12,16},{16,20},{20,24},{24,28},{1,5},{5,9},{9,... | collective-permute-start | bytes 491528 | tf_op jit(solution)/shard_map/ppermute | solution.py:18
  127.7 10.9 %collective-permute-start.13 = (f32[4,2,1,5,4,256]{5,3,4,2,1,0:T(8,128)S(1)}, f32[4,2,1,5,4,256]{5,3,4,2,1,0:T(8,128)S(1)}, u32[]{:S(2)}, u32[]{:S(2)}) collective-permute-start(f32[4,2,1,5,4,256]{5,3,4,2,1,0:T(8,128)S(1)} %get-tuple-element.42), channel_id=1, source_target_pairs={{4,0},{8,4},{12,8},{16,12},{20,16},{24,20},{28,24},{5,1},{9,5},{13... | collective-permute-start | bytes 491528 | tf_op jit(solution)/shard_map/ppermute | solution.py:19
  129.0 15.3 %collective-permute-start.12 = (f32[4,2,1,5,4,256]{5,3,4,2,1,0:T(8,128)S(1)}, f32[4,2,1,5,4,256]{5,3,4,2,1,0:T(8,128)S(1)}, u32[]{:S(2)}, u32[]{:S(2)}) collective-permute-start(f32[4,2,1,5,4,256]{5,3,4,2,1,0:T(8,128)S(1)} %get-tuple-element.43), channel_id=1, source_target_pairs={{0,4},{4,8},{8,12},{12,16},{16,20},{20,24},{24,28},{1,5},{5,9},{9,... | collective-permute-start | bytes 491528 | tf_op jit(solution)/shard_map/ppermute | solution.py:18
  148.2 10.9 %collective-permute-start.15 = (f32[4,2,1,5,4,256]{5,3,4,2,1,0:T(8,128)S(1)}, f32[4,2,1,5,4,256]{5,3,4,2,1,0:T(8,128)S(1)}, u32[]{:S(2)}, u32[]{:S(2)}) collective-permute-start(f32[4,2,1,5,4,256]{5,3,4,2,1,0:T(8,128)S(1)} %get-tuple-element.34), channel_id=1, source_target_pairs={{4,0},{8,4},{12,8},{16,12},{20,16},{24,20},{28,24},{5,1},{9,5},{13... | collective-permute-start | bytes 491528 | tf_op jit(solution)/shard_map/ppermute | solution.py:19
  149.5 15.3 %collective-permute-start.14 = (f32[4,2,1,5,4,256]{5,3,4,2,1,0:T(8,128)S(1)}, f32[4,2,1,5,4,256]{5,3,4,2,1,0:T(8,128)S(1)}, u32[]{:S(2)}, u32[]{:S(2)}) collective-permute-start(f32[4,2,1,5,4,256]{5,3,4,2,1,0:T(8,128)S(1)} %get-tuple-element.35), channel_id=1, source_target_pairs={{0,4},{4,8},{8,12},{12,16},{16,20},{20,24},{24,28},{1,5},{5,9},{9,... | collective-permute-start | bytes 491528 | tf_op jit(solution)/shard_map/ppermute | solution.py:18
  215.5 13.7 %all-to-all-start.1 = ((f32[16,2,4,5,1,256]{5,2,4,3,1,0:T(4,128)}), f32[16,2,4,5,1,256]{5,2,4,3,1,0:T(4,128)S(1)}, u32[]{:S(2)}, u32[]{:S(2)}) async-start(f32[16,2,4,5,1,256]{5,2,4,3,1,0:T(4,128)} %copy.50), calls=%async_computation.1 | async-start | bytes 1310720 | tf_op jit(solution)/shard_map/all_to_all | solution.py:73
where the time goes:
time: 231 us; the launch traced here: 230 us
  waiting for transfers between devices  88.6 us (38%)
  starting transfers between devices  54.9 us (24%)
  blocking collectives  38.7 us (17%)
  matrix products  18.3 us (8%)
  other arithmetic  16 us (7%)
  local copies, waits for them, and re-layouts  12.5 us (5%)
    ppermute x8, waiting for transfers between devices, padded_2(): before = lax.ppermute(last, axis, up)  46.1 us
    ppermute x8, starting transfers between devices, padded_2(): before = lax.ppermute(last, axis, up)  41.1 us
    ppermute x8, waiting for transfers between devices, padded_2(): after = lax.ppermute(leading, axis, down)  33 us
    psum x1, blocking collectives, on_device(): gram = lax.psum(partial_gram, 'gx')  20.1 us
    dot_general x8, matrix products, apply_adjoint(): jnp.einsum('wv,kpxwrt->kpxvrt', coupling, field, precision=lax.Precision....  16.5 us
    all_to_all x1, blocking collectives, on_device(): lax.all_to_all(field, 'af', split_axis=4, concat_axis=0, tiled=True)  12.8 us
    ppermute x8, starting transfers between devices, padded_2(): after = lax.ppermute(leading, axis, down)  10.3 us
    all_to_all x1, waiting for transfers between devices, on_device(): lax.all_to_all(scaled.reshape(regrouped.shape), 'af', split_axis=0, conca...  9.51 us
  transfers between devices with their start and end apart: 17, of which 17 were waited for; matrix products, arithmetic and copies ran while one was open for 1% of the time, Pallas kernels for 0%

commit v1 on v0

--- a/solution.py
+++ b/solution.py
@@ -66,7 +66,8 @@
     total = flat.shape[1] * lax.axis_size("gx") * lax.axis_size("af")
     local_gram = jnp.dot(flat, flat.T, precision=lax.Precision.HIGHEST)
     partial_gram = lax.psum(local_gram, "af")
-    gram = lax.psum(partial_gram, "gx")
+    parts = lax.all_gather(partial_gram, "gx", axis=0, tiled=False)
+    gram = parts.sum(axis=0)
     lower_factor = jnp.linalg.cholesky(gram)
     inverse = jax.scipy.linalg.solve_triangular(lower_factor, eye_matrix, lower=True)
     scaled = jnp.dot(inverse, flat, precision=lax.Precision.HIGHEST) * jnp.sqrt(jnp.float32(total))

time: 231 us -> 242 us (1.048)
  blocking collectives: 38.7 us -> 49.2 us
    all_gather x0 -> x1, blocking collectives: none -> 30.5 us  [on_device(): parts = lax.all_gather(partial_gram, 'gx', axis=0, tiled=False)]
    psum x1 -> x0, blocking collectives: 20.1 us -> none  [on_device(): gram = lax.psum(partial_gram, 'gx')]
where the time goes in v1:
time: 242 us; the launch traced here: 241 us
  waiting for transfers between devices  88.6 us (37%)
  starting transfers between devices  54.9 us (23%)
  blocking collectives  49.2 us (20%)
  matrix products  18.3 us (8%)
  other arithmetic  16 us (7%)
  local copies, waits for them, and re-layouts  12.5 us (5%)
    ppermute x8, waiting for transfers between devices, padded_2(): before = lax.ppermute(last, axis, up)  46.1 us
    ppermute x8, starting transfers between devices, padded_2(): before = lax.ppermute(last, axis, up)  41.1 us
    ppermute x8, waiting for transfers between devices, padded_2(): after = lax.ppermute(leading, axis, down)  33 us
    all_gather x1, blocking collectives, on_device(): parts = lax.all_gather(partial_gram, 'gx', axis=0, tiled=False)  30.5 us
    dot_general x8, matrix products, apply_adjoint(): jnp.einsum('wv,kpxwrt->kpxvrt', coupling, field, precision=lax.Precision....  16.5 us
    all_to_all x1, blocking collectives, on_device(): lax.all_to_all(field, 'af', split_axis=4, concat_axis=0, tiled=True)  12.8 us
    ppermute x8, starting transfers between devices, padded_2(): after = lax.ppermute(leading, axis, down)  10.3 us
    all_to_all x1, waiting for transfers between devices, on_device(): lax.all_to_all(scaled.reshape(regrouped.shape), 'af', split_axis=0, conca...  9.51 us
  transfers between devices with their start and end apart: 17, of which 17 were waited for; matrix products, arithmetic and copies ran while one was open for 1% of the time, Pallas kernels for 0%

profile of v1, /device:TPU:0, one launch (start us, length us, event | category | flops | bytes accessed | tf_op | source)
XLA Modules:
  0.0 241.0 jit_solution(3952928435671190027)
XLA Ops:
  7.8 5.5 %collective-permute-start = (f32[4,2,1,5,4,256]{5,3,4,2,1,0:T(8,128)S(1)}, f32[4,2,1,5,4,256]{5,3,4,2,1,0:T(8,128)S(1)}, u32[]{:S(2)}, u32[]{:S(2)}) collective-permute-start(f32[4,2,1,5,4,256]{5,3,4,2,1,0:T(8,128)S(1)} %get-tuple-element.89), channel_id=1, source_target_pairs={{0,4},{4,8},{8,12},{12,16},{16,20},{20,24},{24,28},{1,5},{5,9},{9,... | collective-permute-start | bytes 491528 | tf_op jit(solution)/shard_map/ppermute | solution.py:18
  17.6 5.8 %collective-permute-done = f32[4,2,1,5,4,256]{5,3,4,2,1,0:T(8,128)S(1)} collective-permute-done((f32[4,2,1,5,4,256]{5,3,4,2,1,0:T(8,128)S(1)}, f32[4,2,1,5,4,256]{5,3,4,2,1,0:T(8,128)S(1)}, u32[]{:S(2)}, u32[]{:S(2)}) %collective-permute-start) | collective-permute-done | bytes 163872 | tf_op jit(solution)/shard_map/ppermute | solution.py:18
  27.9 5.0 %collective-permute-start.2 = (f32[4,2,1,5,4,256]{5,3,4,2,1,0:T(8,128)S(1)}, f32[4,2,1,5,4,256]{5,3,4,2,1,0:T(8,128)S(1)}, u32[]{:S(2)}, u32[]{:S(2)}) collective-permute-start(f32[4,2,1,5,4,256]{5,3,4,2,1,0:T(8,128)S(1)} %get-tuple-element.83), channel_id=1, source_target_pairs={{0,4},{4,8},{8,12},{12,16},{16,20},{20,24},{24,28},{1,5},{5,9},{9,... | collective-permute-start | bytes 491528 | tf_op jit(solution)/shard_map/ppermute | solution.py:18
  37.5 5.8 %collective-permute-done.2 = f32[4,2,1,5,4,256]{5,3,4,2,1,0:T(8,128)S(1)} collective-permute-done((f32[4,2,1,5,4,256]{5,3,4,2,1,0:T(8,128)S(1)}, f32[4,2,1,5,4,256]{5,3,4,2,1,0:T(8,128)S(1)}, u32[]{:S(2)}, u32[]{:S(2)}) %collective-permute-start.2) | collective-permute-done | bytes 163872 | tf_op jit(solution)/shard_map/ppermute | solution.py:18
  47.9 5.0 %collective-permute-start.4 = (f32[4,2,1,5,4,256]{5,3,4,2,1,0:T(8,128)S(1)}, f32[4,2,1,5,4,256]{5,3,4,2,1,0:T(8,128)S(1)}, u32[]{:S(2)}, u32[]{:S(2)}) collective-permute-start(f32[4,2,1,5,4,256]{5,3,4,2,1,0:T(8,128)S(1)} %get-tuple-element.75), channel_id=1, source_target_pairs={{0,4},{4,8},{8,12},{12,16},{16,20},{20,24},{24,28},{1,5},{5,9},{9,... | collective-permute-start | bytes 491528 | tf_op jit(solution)/shard_map/ppermute | solution.py:18
  53.1 4.3 %collective-permute-done.5 = f32[4,2,1,5,4,256]{5,3,4,2,1,0:T(8,128)S(1)} collective-permute-done((f32[4,2,1,5,4,256]{5,3,4,2,1,0:T(8,128)S(1)}, f32[4,2,1,5,4,256]{5,3,4,2,1,0:T(8,128)S(1)}, u32[]{:S(2)}, u32[]{:S(2)}) %collective-permute-start.5) | collective-permute-done | bytes 163872 | tf_op jit(solution)/shard_map/ppermute | solution.py:19
  57.5 5.8 %collective-permute-done.4 = f32[4,2,1,5,4,256]{5,3,4,2,1,0:T(8,128)S(1)} collective-permute-done((f32[4,2,1,5,4,256]{5,3,4,2,1,0:T(8,128)S(1)}, f32[4,2,1,5,4,256]{5,3,4,2,1,0:T(8,128)S(1)}, u32[]{:S(2)}, u32[]{:S(2)}) %collective-permute-start.4) | collective-permute-done | bytes 163872 | tf_op jit(solution)/shard_map/ppermute | solution.py:18
  68.0 5.2 %collective-permute-start.6 = (f32[4,2,1,5,4,256]{5,3,4,2,1,0:T(8,128)S(1)}, f32[4,2,1,5,4,256]{5,3,4,2,1,0:T(8,128)S(1)}, u32[]{:S(2)}, u32[]{:S(2)}) collective-permute-start(f32[4,2,1,5,4,256]{5,3,4,2,1,0:T(8,128)S(1)} %get-tuple-element.67), channel_id=1, source_target_pairs={{0,4},{4,8},{8,12},{12,16},{16,20},{20,24},{24,28},{1,5},{5,9},{9,... | collective-permute-start | bytes 491528 | tf_op jit(solution)/shard_map/ppermute | solution.py:18
  77.6 5.8 %collective-permute-done.6 = f32[4,2,1,5,4,256]{5,3,4,2,1,0:T(8,128)S(1)} collective-permute-done((f32[4,2,1,5,4,256]{5,3,4,2,1,0:T(8,128)S(1)}, f32[4,2,1,5,4,256]{5,3,4,2,1,0:T(8,128)S(1)}, u32[]{:S(2)}, u32[]{:S(2)}) %collective-permute-start.6) | collective-permute-done | bytes 163872 | tf_op jit(solution)/shard_map/ppermute | solution.py:18
  88.2 5.0 %collective-permute-start.8 = (f32[4,2,1,5,4,256]{5,3,4,2,1,0:T(8,128)S(1)}, f32[4,2,1,5,4,256]{5,3,4,2,1,0:T(8,128)S(1)}, u32[]{:S(2)}, u32[]{:S(2)}) collective-permute-start(f32[4,2,1,5,4,256]{5,3,4,2,1,0:T(8,128)S(1)} %get-tuple-element.59), channel_id=1, source_target_pairs={{0,4},{4,8},{8,12},{12,16},{16,20},{20,24},{24,28},{1,5},{5,9},{9,... | collective-permute-start | bytes 491528 | tf_op jit(solution)/shard_map/ppermute | solution.py:18
  93.5 4.3 %collective-permute-done.9 = f32[4,2,1,5,4,256]{5,3,4,2,1,0:T(8,128)S(1)} collective-permute-done((f32[4,2,1,5,4,256]{5,3,4,2,1,0:T(8,128)S(1)}, f32[4,2,1,5,4,256]{5,3,4,2,1,0:T(8,128)S(1)}, u32[]{:S(2)}, u32[]{:S(2)}) %collective-permute-start.9) | collective-permute-done | bytes 163872 | tf_op jit(solution)/shard_map/ppermute | solution.py:19
  97.8 5.8 %collective-permute-done.8 = f32[4,2,1,5,4,256]{5,3,4,2,1,0:T(8,128)S(1)} collective-permute-done((f32[4,2,1,5,4,256]{5,3,4,2,1,0:T(8,128)S(1)}, f32[4,2,1,5,4,256]{5,3,4,2,1,0:T(8,128)S(1)}, u32[]{:S(2)}, u32[]{:S(2)}) %collective-permute-start.8) | collective-permute-done | bytes 163872 | tf_op jit(solution)/shard_map/ppermute | solution.py:18
  108.6 5.0 %collective-permute-start.10 = (f32[4,2,1,5,4,256]{5,3,4,2,1,0:T(8,128)S(1)}, f32[4,2,1,5,4,256]{5,3,4,2,1,0:T(8,128)S(1)}, u32[]{:S(2)}, u32[]{:S(2)}) collective-permute-start(f32[4,2,1,5,4,256]{5,3,4,2,1,0:T(8,128)S(1)} %get-tuple-element.51), channel_id=1, source_target_pairs={{0,4},{4,8},{8,12},{12,16},{16,20},{20,24},{24,28},{1,5},{5,9},{9,... | collective-permute-start | bytes 491528 | tf_op jit(solution)/shard_map/ppermute | solution.py:18
  113.8 4.3 %collective-permute-done.11 = f32[4,2,1,5,4,256]{5,3,4,2,1,0:T(8,128)S(1)} collective-permute-done((f32[4,2,1,5,4,256]{5,3,4,2,1,0:T(8,128)S(1)}, f32[4,2,1,5,4,256]{5,3,4,2,1,0:T(8,128)S(1)}, u32[]{:S(2)}, u32[]{:S(2)}) %collective-permute-start.11) | collective-permute-done | bytes 163872 | tf_op jit(solution)/shard_map/ppermute | solution.py:19
  118.1 5.8 %collective-permute-done.10 = f32[4,2,1,5,4,256]{5,3,4,2,1,0:T(8,128)S(1)} collective-permute-done((f32[4,2,1,5,4,256]{5,3,4,2,1,0:T(8,128)S(1)}, f32[4,2,1,5,4,256]{5,3,4,2,1,0:T(8,128)S(1)}, u32[]{:S(2)}, u32[]{:S(2)}) %collective-permute-start.10) | collective-permute-done | bytes 163872 | tf_op jit(solution)/shard_map/ppermute | solution.py:18
  129.0 5.2 %collective-permute-start.12 = (f32[4,2,1,5,4,256]{5,3,4,2,1,0:T(8,128)S(1)}, f32[4,2,1,5,4,256]{5,3,4,2,1,0:T(8,128)S(1)}, u32[]{:S(2)}, u32[]{:S(2)}) collective-permute-start(f32[4,2,1,5,4,256]{5,3,4,2,1,0:T(8,128)S(1)} %get-tuple-element.43), channel_id=1, source_target_pairs={{0,4},{4,8},{8,12},{12,16},{16,20},{20,24},{24,28},{1,5},{5,9},{9,... | collective-permute-start | bytes 491528 | tf_op jit(solution)/shard_map/ppermute | solution.py:18
  138.6 5.8 %collective-permute-done.12 = f32[4,2,1,5,4,256]{5,3,4,2,1,0:T(8,128)S(1)} collective-permute-done((f32[4,2,1,5,4,256]{5,3,4,2,1,0:T(8,128)S(1)}, f32[4,2,1,5,4,256]{5,3,4,2,1,0:T(8,128)S(1)}, u32[]{:S(2)}, u32[]{:S(2)}) %collective-permute-start.12) | collective-permute-done | bytes 163872 | tf_op jit(solution)/shard_map/ppermute | solution.py:18
  149.5 5.0 %collective-permute-start.14 = (f32[4,2,1,5,4,256]{5,3,4,2,1,0:T(8,128)S(1)}, f32[4,2,1,5,4,256]{5,3,4,2,1,0:T(8,128)S(1)}, u32[]{:S(2)}, u32[]{:S(2)}) collective-permute-start(f32[4,2,1,5,4,256]{5,3,4,2,1,0:T(8,128)S(1)} %get-tuple-element.35), channel_id=1, source_target_pairs={{0,4},{4,8},{8,12},{12,16},{16,20},{20,24},{24,28},{1,5},{5,9},{9,... | collective-permute-start | bytes 491528 | tf_op jit(solution)/shard_map/ppermute | solution.py:18
  154.8 4.3 %collective-permute-done.15 = f32[4,2,1,5,4,256]{5,3,4,2,1,0:T(8,128)S(1)} collective-permute-done((f32[4,2,1,5,4,256]{5,3,4,2,1,0:T(8,128)S(1)}, f32[4,2,1,5,4,256]{5,3,4,2,1,0:T(8,128)S(1)}, u32[]{:S(2)}, u32[]{:S(2)}) %collective-permute-start.15) | collective-permute-done | bytes 163872 | tf_op jit(solution)/shard_map/ppermute | solution.py:19
  159.1 5.8 %collective-permute-done.14 = f32[4,2,1,5,4,256]{5,3,4,2,1,0:T(8,128)S(1)} collective-permute-done((f32[4,2,1,5,4,256]{5,3,4,2,1,0:T(8,128)S(1)}, f32[4,2,1,5,4,256]{5,3,4,2,1,0:T(8,128)S(1)}, u32[]{:S(2)}, u32[]{:S(2)}) %collective-permute-start.14) | collective-permute-done | bytes 163872 | tf_op jit(solution)/shard_map/ppermute | solution.py:18
  168.9 12.8 %all_to_all.33 = f32[4,2,4,5,4,256]{5,2,3,1,0,4:T(4,128)S(1)} all-to-all(f32[4,2,4,5,4,256]{5,2,3,1,0,4:T(4,128)S(1)} %copy.44), channel_id=1, replica_groups=mesh['gx'=8,'af'=4] {'af'}, dimensions={4} | all-to-all | bytes 1310720 | tf_op jit(solution)/shard_map/all_to_all | solution.py:64
  183.2 5.9 %psum.7 = f32[1,16,16]{2,1,0:T(8,128)S(1)} all-reduce(f32[1,16,16]{2,1,0:T(8,128)S(1)} %convolution_bitcast_fusion.8), channel_id=1, replica_groups=mesh['gx'=8,'af'=4] {'af'}, use_global_device_ids=true, to_apply=%region_0.1 | all-reduce | flops 256 | bytes 2048 | tf_op jit(solution)/shard_map/psum | solution.py:68
  189.0 30.5 %all_gather.7 = f32[8,16,16]{2,1,0:T(8,128)S(1)} all-gather(f32[1,16,16]{2,1,0:T(8,128)S(1)} %psum.7), channel_id=1, replica_groups=mesh['gx'=8,'af'=4] {'gx'}, dimensions={0}, use_global_device_ids=true | all-gather | bytes 9216 | tf_op jit(solution)/shard_map/all_gather | solution.py:69
  230.2 9.5 %all-to-all-done.1 = f32[16,2,4,5,1,256]{5,2,4,3,1,0:T(4,128)S(1)} async-done(((f32[16,2,4,5,1,256]{5,2,4,3,1,0:T(4,128)}), f32[16,2,4,5,1,256]{5,2,4,3,1,0:T(4,128)S(1)}, u32[]{:S(2)}, u32[]{:S(2)}) %all-to-all-start.1) | async-done | bytes 655392 | tf_op jit(solution)/shard_map/all_to_all | solution.py:74
  (105 shorter events, 76.4 us)
Async XLA Ops:
  0.6 4.7 %copy-start = (f32[5,5]{1,0:T(8,128)S(1)}, f32[5,5]{1,0:T(8,128)}, u32[]{:S(2)}) copy-start(f32[5,5]{1,0:T(8,128)} %param.8) | copy-start | bytes 304
  6.5 11.2 %collective-permute-start.1 = (f32[4,2,1,5,4,256]{5,3,4,2,1,0:T(8,128)S(1)}, f32[4,2,1,5,4,256]{5,3,4,2,1,0:T(8,128)S(1)}, u32[]{:S(2)}, u32[]{:S(2)}) collective-permute-start(f32[4,2,1,5,4,256]{5,3,4,2,1,0:T(8,128)S(1)} %get-tuple-element.88), channel_id=1, source_target_pairs={{4,0},{8,4},{12,8},{16,12},{20,16},{24,20},{28,24},{5,1},{9,5},{13... | collective-permute-start | bytes 491528 | tf_op jit(solution)/shard_map/ppermute | solution.py:19
  7.8 15.6 %collective-permute-start = (f32[4,2,1,5,4,256]{5,3,4,2,1,0:T(8,128)S(1)}, f32[4,2,1,5,4,256]{5,3,4,2,1,0:T(8,128)S(1)}, u32[]{:S(2)}, u32[]{:S(2)}) collective-permute-start(f32[4,2,1,5,4,256]{5,3,4,2,1,0:T(8,128)S(1)} %get-tuple-element.89), channel_id=1, source_target_pairs={{0,4},{4,8},{8,12},{12,16},{16,20},{20,24},{24,28},{1,5},{5,9},{9,... | collective-permute-start | bytes 491528 | tf_op jit(solution)/shard_map/ppermute | solution.py:18
  13.4 0.7 copy-start.2
  14.1 9.3 %copy-start.1 = (f32[4,2,4,5,4,256]{5,4,3,2,1,0:T(4,128)S(1)}, f32[4,2,4,5,4,256]{5,4,3,2,1,0:T(4,128)}, u32[]{:S(2)}) copy-start(f32[4,2,4,5,4,256]{5,4,3,2,1,0:T(4,128)} %param.5) | copy-start | bytes 1966084
  14.1 9.3 %copy-start.3 = (f32[4,4,256]{2,1,0:T(4,128)S(1)}, f32[4,4,256]{2,1,0:T(4,128)}, u32[]{:S(2)}) copy-start(f32[4,4,256]{2,1,0:T(4,128)} %param.7) | copy-start | bytes 49156
  26.6 10.9 %collective-permute-start.3 = (f32[4,2,1,5,4,256]{5,3,4,2,1,0:T(8,128)S(1)}, f32[4,2,1,5,4,256]{5,3,4,2,1,0:T(8,128)S(1)}, u32[]{:S(2)}, u32[]{:S(2)}) collective-permute-start(f32[4,2,1,5,4,256]{5,3,4,2,1,0:T(8,128)S(1)} %get-tuple-element.82), channel_id=1, source_target_pairs={{4,0},{8,4},{12,8},{16,12},{20,16},{24,20},{28,24},{5,1},{9,5},{13... | collective-permute-start | bytes 491528 | tf_op jit(solution)/shard_map/ppermute | solution.py:19
  27.9 15.3 %collective-permute-start.2 = (f32[4,2,1,5,4,256]{5,3,4,2,1,0:T(8,128)S(1)}, f32[4,2,1,5,4,256]{5,3,4,2,1,0:T(8,128)S(1)}, u32[]{:S(2)}, u32[]{:S(2)}) collective-permute-start(f32[4,2,1,5,4,256]{5,3,4,2,1,0:T(8,128)S(1)} %get-tuple-element.83), channel_id=1, source_target_pairs={{0,4},{4,8},{8,12},{12,16},{16,20},{20,24},{24,28},{1,5},{5,9},{9,... | collective-permute-start | bytes 491528 | tf_op jit(solution)/shard_map/ppermute | solution.py:18
  46.6 10.9 %collective-permute-start.5 = (f32[4,2,1,5,4,256]{5,3,4,2,1,0:T(8,128)S(1)}, f32[4,2,1,5,4,256]{5,3,4,2,1,0:T(8,128)S(1)}, u32[]{:S(2)}, u32[]{:S(2)}) collective-permute-start(f32[4,2,1,5,4,256]{5,3,4,2,1,0:T(8,128)S(1)} %get-tuple-element.74), channel_id=1, source_target_pairs={{4,0},{8,4},{12,8},{16,12},{20,16},{24,20},{28,24},{5,1},{9,5},{13... | collective-permute-start | bytes 491528 | tf_op jit(solution)/shard_map/ppermute | solution.py:19
  47.9 15.3 %collective-permute-start.4 = (f32[4,2,1,5,4,256]{5,3,4,2,1,0:T(8,128)S(1)}, f32[4,2,1,5,4,256]{5,3,4,2,1,0:T(8,128)S(1)}, u32[]{:S(2)}, u32[]{:S(2)}) collective-permute-start(f32[4,2,1,5,4,256]{5,3,4,2,1,0:T(8,128)S(1)} %get-tuple-element.75), channel_id=1, source_target_pairs={{0,4},{4,8},{8,12},{12,16},{16,20},{20,24},{24,28},{1,5},{5,9},{9,... | collective-permute-start | bytes 491528 | tf_op jit(solution)/shard_map/ppermute | solution.py:18
  66.7 10.9 %collective-permute-start.7 = (f32[4,2,1,5,4,256]{5,3,4,2,1,0:T(8,128)S(1)}, f32[4,2,1,5,4,256]{5,3,4,2,1,0:T(8,128)S(1)}, u32[]{:S(2)}, u32[]{:S(2)}) collective-permute-start(f32[4,2,1,5,4,256]{5,3,4,2,1,0:T(8,128)S(1)} %get-tuple-element.66), channel_id=1, source_target_pairs={{4,0},{8,4},{12,8},{16,12},{20,16},{24,20},{28,24},{5,1},{9,5},{13... | collective-permute-start | bytes 491528 | tf_op jit(solution)/shard_map/ppermute | solution.py:19
  68.0 15.3 %collective-permute-start.6 = (f32[4,2,1,5,4,256]{5,3,4,2,1,0:T(8,128)S(1)}, f32[4,2,1,5,4,256]{5,3,4,2,1,0:T(8,128)S(1)}, u32[]{:S(2)}, u32[]{:S(2)}) collective-permute-start(f32[4,2,1,5,4,256]{5,3,4,2,1,0:T(8,128)S(1)} %get-tuple-element.67), channel_id=1, source_target_pairs={{0,4},{4,8},{8,12},{12,16},{16,20},{20,24},{24,28},{1,5},{5,9},{9,... | collective-permute-start | bytes 491528 | tf_op jit(solution)/shard_map/ppermute | solution.py:18
  86.9 10.9 %collective-permute-start.9 = (f32[4,2,1,5,4,256]{5,3,4,2,1,0:T(8,128)S(1)}, f32[4,2,1,5,4,256]{5,3,4,2,1,0:T(8,128)S(1)}, u32[]{:S(2)}, u32[]{:S(2)}) collective-permute-start(f32[4,2,1,5,4,256]{5,3,4,2,1,0:T(8,128)S(1)} %get-tuple-element.58), channel_id=1, source_target_pairs={{4,0},{8,4},{12,8},{16,12},{20,16},{24,20},{28,24},{5,1},{9,5},{13... | collective-permute-start | bytes 491528 | tf_op jit(solution)/shard_map/ppermute | solution.py:19
  88.2 15.3 %collective-permute-start.8 = (f32[4,2,1,5,4,256]{5,3,4,2,1,0:T(8,128)S(1)}, f32[4,2,1,5,4,256]{5,3,4,2,1,0:T(8,128)S(1)}, u32[]{:S(2)}, u32[]{:S(2)}) collective-permute-start(f32[4,2,1,5,4,256]{5,3,4,2,1,0:T(8,128)S(1)} %get-tuple-element.59), channel_id=1, source_target_pairs={{0,4},{4,8},{8,12},{12,16},{16,20},{20,24},{24,28},{1,5},{5,9},{9,... | collective-permute-start | bytes 491528 | tf_op jit(solution)/shard_map/ppermute | solution.py:18
  107.3 10.9 %collective-permute-start.11 = (f32[4,2,1,5,4,256]{5,3,4,2,1,0:T(8,128)S(1)}, f32[4,2,1,5,4,256]{5,3,4,2,1,0:T(8,128)S(1)}, u32[]{:S(2)}, u32[]{:S(2)}) collective-permute-start(f32[4,2,1,5,4,256]{5,3,4,2,1,0:T(8,128)S(1)} %get-tuple-element.50), channel_id=1, source_target_pairs={{4,0},{8,4},{12,8},{16,12},{20,16},{24,20},{28,24},{5,1},{9,5},{13... | collective-permute-start | bytes 491528 | tf_op jit(solution)/shard_map/ppermute | solution.py:19
  108.6 15.3 %collective-permute-start.10 = (f32[4,2,1,5,4,256]{5,3,4,2,1,0:T(8,128)S(1)}, f32[4,2,1,5,4,256]{5,3,4,2,1,0:T(8,128)S(1)}, u32[]{:S(2)}, u32[]{:S(2)}) collective-permute-start(f32[4,2,1,5,4,256]{5,3,4,2,1,0:T(8,128)S(1)} %get-tuple-element.51), channel_id=1, source_target_pairs={{0,4},{4,8},{8,12},{12,16},{16,20},{20,24},{24,28},{1,5},{5,9},{9,... | collective-permute-start | bytes 491528 | tf_op jit(solution)/shard_map/ppermute | solution.py:18
  127.7 10.9 %collective-permute-start.13 = (f32[4,2,1,5,4,256]{5,3,4,2,1,0:T(8,128)S(1)}, f32[4,2,1,5,4,256]{5,3,4,2,1,0:T(8,128)S(1)}, u32[]{:S(2)}, u32[]{:S(2)}) collective-permute-start(f32[4,2,1,5,4,256]{5,3,4,2,1,0:T(8,128)S(1)} %get-tuple-element.42), channel_id=1, source_target_pairs={{4,0},{8,4},{12,8},{16,12},{20,16},{24,20},{28,24},{5,1},{9,5},{13... | collective-permute-start | bytes 491528 | tf_op jit(solution)/shard_map/ppermute | solution.py:19
  129.0 15.3 %collective-permute-start.12 = (f32[4,2,1,5,4,256]{5,3,4,2,1,0:T(8,128)S(1)}, f32[4,2,1,5,4,256]{5,3,4,2,1,0:T(8,128)S(1)}, u32[]{:S(2)}, u32[]{:S(2)}) collective-permute-start(f32[4,2,1,5,4,256]{5,3,4,2,1,0:T(8,128)S(1)} %get-tuple-element.43), channel_id=1, source_target_pairs={{0,4},{4,8},{8,12},{12,16},{16,20},{20,24},{24,28},{1,5},{5,9},{9,... | collective-permute-start | bytes 491528 | tf_op jit(solution)/shard_map/ppermute | solution.py:18
  148.2 10.9 %collective-permute-start.15 = (f32[4,2,1,5,4,256]{5,3,4,2,1,0:T(8,128)S(1)}, f32[4,2,1,5,4,256]{5,3,4,2,1,0:T(8,128)S(1)}, u32[]{:S(2)}, u32[]{:S(2)}) collective-permute-start(f32[4,2,1,5,4,256]{5,3,4,2,1,0:T(8,128)S(1)} %get-tuple-element.34), channel_id=1, source_target_pairs={{4,0},{8,4},{12,8},{16,12},{20,16},{24,20},{28,24},{5,1},{9,5},{13... | collective-permute-start | bytes 491528 | tf_op jit(solution)/shard_map/ppermute | solution.py:19
  149.5 15.3 %collective-permute-start.14 = (f32[4,2,1,5,4,256]{5,3,4,2,1,0:T(8,128)S(1)}, f32[4,2,1,5,4,256]{5,3,4,2,1,0:T(8,128)S(1)}, u32[]{:S(2)}, u32[]{:S(2)}) collective-permute-start(f32[4,2,1,5,4,256]{5,3,4,2,1,0:T(8,128)S(1)} %get-tuple-element.35), channel_id=1, source_target_pairs={{0,4},{4,8},{8,12},{12,16},{16,20},{20,24},{24,28},{1,5},{5,9},{9,... | collective-permute-start | bytes 491528 | tf_op jit(solution)/shard_map/ppermute | solution.py:18
  226.0 13.7 %all-to-all-start.1 = ((f32[16,2,4,5,1,256]{5,2,4,3,1,0:T(4,128)}), f32[16,2,4,5,1,256]{5,2,4,3,1,0:T(4,128)S(1)}, u32[]{:S(2)}, u32[]{:S(2)}) async-start(f32[16,2,4,5,1,256]{5,2,4,3,1,0:T(4,128)} %copy.47), calls=%async_computation.1 | async-start | bytes 1310720 | tf_op jit(solution)/shard_map/all_to_all | solution.py:74
